TPU v7x, 512 devices: a whole 4x8x8 slice. The times are simulated.
512 devices in a mesh: row: 16 (over z, y_lo), col: 32 (over x, y_hi, core).
Axes of the slice: x: 4, y: 8 (y_hi: 4, y_lo: 2; y = y_hi * 2 + y_lo), z: 8, core: 2. Of those that a mesh axis runs over, the one named last changes fastest.
Arguments:
- contribution: float32 [4096, 24576], P('row', 'col'), may hold values from -6 to 6
- left_basis: bfloat16 [8, 32, 64, 4096], P(None, 'col', None, 'row'), may hold values from -6 to 6
- left_coef: bfloat16 [8, 32, 64, 4096], P(None, 'col', None, 'row'), may hold values from -0.75 to 0.75
- right_coef: bfloat16 [8, 16, 64, 8192], P(None, 'row', None, 'col'), may hold values from -0.75 to 0.75
- right_basis: bfloat16 [8, 16, 64, 24576], P(None, 'row', None, 'col'), may hold values from -6 to 6
- left_rank: int32 [8, 16], P(None, 'row'), may hold values from 8 to 64
- left_scale: float32 [8, 16], P(None, 'row'), may hold values from 0.08 to 0.8
- right_rank: int32 [8, 32], P(None, 'col'), may hold values from 8 to 64
- right_scale: float32 [8, 32], P(None, 'col'), may hold values from 0.08 to 0.8
- left_owner: int32 [8], replicated, may hold values from 0 to 31
- right_owner: int32 [8], replicated, may hold values from 0 to 15
Outputs:
- updated: float32 [4096, 24576], P('row', 'col')
All inputs are finite; a program needn't handle non-finite values.
Results may differ from a plain program's by a relative error of at most 0.0003.
Values may be sent and summed in bfloat16 or wider, within the bound.
A program may use at most 64 MiB of HBM per device.

v0:
```python
import jax
import jax.numpy as jnp
from jax import lax
from jax.sharding import PartitionSpec as P


def spread(x, axis, root):
    mine = lax.axis_index(axis) == root
    return lax.psum(jnp.where(mine, x, jnp.zeros_like(x)), axis)


def first_low(left, right):
    return lax.dot_general(
        left, right, (((0,), (0,)), ((), ())), preferred_element_type=jnp.float32
    )


def plain_high(left, right):
    return jnp.dot(left, right, precision=lax.Precision.HIGHEST)


def shards(
    contribution,
    left_basis,
    left_coef,
    right_coef,
    right_basis,
    left_rank,
    left_scale,
    right_rank,
    right_scale,
    left_owner,
    right_owner,
):
    panels = left_basis.shape[0]
    rmax = left_basis.shape[2]
    slots = jnp.arange(rmax)
    lkeep = slots[None, :] < left_rank
    rkeep = slots[None, :] < right_rank
    zero_half = jnp.zeros((), jnp.bfloat16)
    total = jnp.zeros(contribution.shape, jnp.float32)
    for panel in range(panels):
        lbasis, lcoef = (
            spread(left_basis[panel, 0], "col", left_owner[panel]),
            spread(left_coef[panel, 0], "col", left_owner[panel]),
        )
        rcoef, rbasis = (
            spread(right_coef[panel, 0], "row", right_owner[panel]),
            spread(right_basis[panel, 0], "row", right_owner[panel]),
        )
        lmasked = jnp.where(lkeep[panel][:, None], lbasis, zero_half)
        rmasked = jnp.where(rkeep[panel][:, None], rcoef, zero_half)
        lfactor = left_scale[panel, 0]
        rfactor = right_scale[panel, 0]
        left_tile = first_low(lmasked, lcoef) * lfactor
        right_tile = first_low(rmasked, rbasis) * rfactor
        total = total + plain_high(left_tile, right_tile)
    return contribution - total


def solution(mesh):
    return jax.shard_map(
        shards,
        mesh=mesh,
        in_specs=(
            P("row", "col"),
            P(None, "col", None, "row"),
            P(None, "col", None, "row"),
            P(None, "row", None, "col"),
            P(None, "row", None, "col"),
            P(None, "row"),
            P(None, "row"),
            P(None, "col"),
            P(None, "col"),
            P(),
            P(),
        ),
        out_specs=P("row", "col"),
        check_vma=False,
    )
```

profile of v0, /device:TPU:2, one launch (start us, length us, event | category | flops | bytes accessed | tf_op | source)
XLA Modules:
  0.0 633.0 jit_solution(3445625677545302321)
XLA Ops:
  13.0 1.6 select_bitcast_fusion.9
  22.0 0.9 select_bitcast_fusion
  26.4 274.7 %all-reduce.7.cloned.1.call-done = (bf16[64,256]{1,0:T(8,128)(2,1)}, bf16[64,256]{1,0:T(8,128)(2,1)}, bf16[64,256]{1,0:T(8,128)(2,1)}, bf16[64,256]{1,0:T(8,128)...) async-done(((bf16[64,256]{1,0:T(8,128)(2,1)}, ...) | async-done | bytes 524304 | tf_op jit(solution)/shard_map/psum | solution.py:9
  301.1 1.7 convolution_multiply_fusion.15
  302.9 0.9 convolution_multiply_fusion.14
  303.8 0.9 convolution_multiply_fusion.13
  304.7 1.0 convolution_multiply_fusion.12
  305.8 0.9 convolution_multiply_fusion.11
  306.7 1.0 convolution_multiply_fusion.10
  307.7 0.8 convolution_multiply_fusion.9
  308.6 0.9 convolution_multiply_fusion.8
  309.5 150.9 %all-reduce.9.cloned.1.call-done = (bf16[64,256]{1,0:T(8,128)(2,1)}, bf16[64,256]{1,0:T(8,128)(2,1)}, bf16[64,256]{1,0:T(8,128)(2,1)}, bf16[64,256]{1,0:T(8,128)...) async-done(((bf16[64,256]{1,0:T(8,128)(2,1)}, bf16[64,256]{1,0:T(8,128)(2,1)}, ...) | async-done | bytes 262160 | tf_op jit(solution)/shard_map/psum | solution.py:9
  460.4 149.2 %all-reduce.11.cloned.1.call-done = (bf16[64,768]{1,0:T(8,128)(2,1)}, bf16[64,768]{1,0:T(8,128)(2,1)}, bf16[64,768]{1,0:T(8,128)(2,1)}, bf16[64,768]{1,0:T(8,128...) async-done(((bf16[64,768]{1,0:T(8,128)(2,1)}, bf16[64,768]{1,0:T(8,128)(2,1)}, ...) | async-done | bytes 786448 | tf_op jit(solution)/shard_map/psum | solution.py:9
  609.6 1.9 convolution_multiply_fusion.7
  611.6 0.8 fusion.69
  612.4 1.0 convolution_multiply_fusion.6
  614.3 1.0 convolution_multiply_fusion.5
  615.4 0.8 convolution_add_fusion.5
  616.2 1.0 convolution_multiply_fusion.4
  618.1 0.9 convolution_multiply_fusion.3
  619.9 1.0 convolution_multiply_fusion.2
  621.8 1.0 convolution_multiply_fusion.1
  623.7 1.0 convolution_multiply_fusion
  624.8 1.7 fusion
  (97 shorter events, 11.7 us)
Async XLA Ops:
  6.5 294.6 %all-reduce.7.cloned.1.call-start = ((), (), s32[]{:S(2)}) async-start(), calls=%async_computation | async-start | bytes 1048576 | tf_op jit(solution)/shard_map/psum | solution.py:9
  13.0 1.7 copy-start.2
  14.6 6.6 %copy-start.3 = (bf16[8,1,64,256]{3,2,1,0:T(8,128)(2,1)S(1)}, bf16[8,1,64,256]{3,2,1,0:T(8,128)(2,1)}, u32[]{:S(2)}) copy-start(bf16[8,1,64,256]{3,2,1,0:T(8,128)(2,1)} %param.14) | copy-start | bytes 786436
  15.4 6.6 %copy-start = (bf16[8,1,64,768]{3,2,1,0:T(8,128)(2,1)S(1)}, bf16[8,1,64,768]{3,2,1,0:T(8,128)(2,1)}, u32[]{:S(2)}) copy-start(bf16[8,1,64,768]{3,2,1,0:T(8,128)(2,1)} %param.15) | copy-start | bytes 2359300
  15.4 445.1 %all-reduce.9.cloned.1.call-start = ((), (), s32[]{:S(2)}) async-start(), calls=%async_computation.1 | async-start | bytes 524288 | tf_op jit(solution)/shard_map/psum | solution.py:9
  22.0 587.7 %all-reduce.11.cloned.1.call-start = ((), (), s32[]{:S(2)}) async-start(), calls=%async_computation.2 | async-start | bytes 1572864 | tf_op jit(solution)/shard_map/psum | solution.py:9
  22.9 2.1 copy-start.35
  301.1 1.7 copy-start.30
  301.1 1.7 copy-start.31
  303.7 1.0 copy-start.25
  303.7 1.0 copy-start.26
  304.7 1.0 copy-start.23
  304.7 1.0 copy-start.24
  305.7 0.9 copy-start.20
  305.7 0.9 copy-start.21
  306.7 1.0 copy-start.18
  306.7 1.0 copy-start.19
  611.5 0.9 copy-start.10
  613.4 0.9 copy-start.9
  615.3 0.9 copy-start.8
  617.2 0.9 copy-start.7
  619.0 0.9 copy-start.6
  620.9 0.9 copy-start.5
  623.7 1.1 copy-start.1
  (17 other events, 14.1 us)
Sparse Core Ops, SparseCore 0:
  15.5 285.5 all-reduce.6
  304.6 155.7 all-reduce.8
  463.9 145.6 all-reduce.10
where the time goes:
time: 634 us; the launch traced here: 633 us
  waiting for transfers between devices  575 us (91%)
  matrix products  24.3 us (4%)
  between operations  23.8 us (4%)
    psum x3, waiting for transfers between devices, spread(): return lax.psum(jnp.where(mine, x, jnp.zeros_like(x)), axis)  575 us
    dot_general x16, matrix products, first_low(): lax.dot_general(left, right, (((0,), (0,)), ((), ())), preferred_element_...  16.8 us
  transfers between devices with their start and end apart: 3, of which 3 were waited for; matrix products, arithmetic and copies ran while one was open for 2% of the time, Pallas kernels for 0%

commit v1 on v0

v1 whole, which is shorter than its diff:
```python
import jax
import jax.numpy as jnp
from jax import lax
from jax.experimental import pallas as pl
from jax.experimental.pallas import tpu as pltpu
from jax.sharding import PartitionSpec as P

MESH = pl.DeviceIdType.MESH
BF16, F32 = jnp.bfloat16, jnp.float32
PANELS, RANK, WIDE = 8, 64, 256
ROWS_OUT, COLS_OUT = 256, 768
ZS, XS, HS = 8, 4, 4
N_SEND, N_RECV = 112, 112


def ring(value, size):
    return lax.rem(value + 4 * size, size)


def flat_dot(left, right, dims):
    return lax.dot_general(left, right, (dims, ((), ())), preferred_element_type=F32)


def split(value):
    high = value.astype(BF16)
    return high, (value - high.astype(F32)).astype(BF16)


def kernel(
    lowner, rowner, lrank, lscale, rrank, rscale,
    lbasis, lcoef, rcoef, rbasis,
    out,
    own, from_lo, from_hi, right, yswap, yhold,
    lown, lother, lpick, lx, lhome, ly, lquarter, left,
    mid_high, mid_low,
    load_sem, send_sem, recv_sem,
):
    row, col = lax.axis_index("row"), lax.axis_index("col")
    z, q = row // 2, lax.rem(row, 2)
    x, h, core = col // 8, lax.rem(col // 2, 4), lax.rem(col, 2)

    def at_row(zz, qq):
        return (zz * 2 + qq, col)

    def at_col(xx, hh, cc):
        return (row, (xx * 4 + hh) * 2 + cc)

    z_up, z_dn = at_row(ring(z + 1, ZS), q), at_row(ring(z - 1, ZS), q)
    y_mate, core_mate = at_row(z, 1 - q), at_col(x, h, 1 - core)
    x_peers = [at_col(ring(x + d, XS), h, core) for d in (1, 2, 3)]
    h_peers = [at_col(x, ring(h + d, HS), core) for d in (1, 2, 3)]
    everyone = [z_up, z_dn, y_mate, core_mate] + x_peers + h_peers

    loads = [
        pltpu.make_async_copy(rcoef.at[:, 0], own.at[:, 0], load_sem.at[0]),
        pltpu.make_async_copy(lbasis.at[:, 0], lown.at[0], load_sem.at[4]),
        pltpu.make_async_copy(lcoef.at[:, 0], lown.at[1], load_sem.at[5]),
    ] + [
        pltpu.make_async_copy(
            rbasis.at[:, 0, :, pl.ds(WIDE * (u - 1), WIDE)], own.at[:, u], load_sem.at[u]
        )
        for u in (1, 2, 3)
    ]
    for load in loads:
        load.start()

    barrier = pltpu.get_barrier_semaphore()
    for peer in everyone:
        pl.semaphore_signal(barrier, inc=1, device_id=peer, device_id_type=MESH)
    pl.semaphore_wait(barrier, len(everyone))
    for load in loads:
        load.wait()

    sent, slots = [], {}

    def send(src, dst, key, peer):
        slot = slots.setdefault(key, len(slots))
        copy = pltpu.make_async_remote_copy(
            src_ref=src, dst_ref=dst, send_sem=send_sem.at[len(sent)],
            recv_sem=recv_sem.at[slot], device_id=peer, device_id_type=MESH,
        )
        copy.start()
        sent.append(copy)

    def arrived(dst, key):
        slot = slots.setdefault(key, len(slots))
        pltpu.make_async_remote_copy(
            src_ref=dst, dst_ref=dst, send_sem=send_sem.at[0],
            recv_sem=recv_sem.at[slot], device_id=core_mate, device_id_type=MESH,
        ).wait_recv()

    units = [2 * (1 - q), 2 * (1 - q) + 1, 2 * q, 2 * q + 1]

    def collect(u, step):
        odd = u % 2
        for up in (True, False):
            long = (odd == 0) == up
            if step == 1 and not long:
                continue
            bufs = from_lo if up else from_hi
            panel = ring(z + (5 - step if up else step - 5), ZS)
            peer = z_up if up else z_dn
            target = bufs.at[step - 1, u]
            if step == 1 or (step == 2 and not long):
                send(own.at[panel, units[u]], target, ("c", up, step, u), peer)
            else:
                held = bufs.at[step - 2, u]
                arrived(held, ("c", up, step - 1, u))
                mine = rowner[panel] // 2 == z
                held[...] = jnp.where(mine, own[panel, units[u]], held[...])
                send(held, target, ("c", up, step, u), peer)

    def home(u):
        arrived(from_lo.at[3, u], ("c", True, 4, u))
        arrived(from_hi.at[3, u], ("c", False, 4, u))
        far = ring(rowner[z] // 2 - z, ZS)
        limit = 4 if u % 2 == 0 else 5
        picked = jnp.where(far >= limit, from_lo[3, u], from_hi[3, u])
        picked = jnp.where(far == 0, own[z, units[u]], picked)
        e = u % 2
        if u < 2:
            yhold[e] = picked
            send(yhold.at[e], yswap.at[e], ("y", e), y_mate)
        else:
            arrived(yswap.at[e], ("y", e))
            right[z, units[u]] = jnp.where(lax.rem(rowner[z], 2) == q, picked, yswap[e])
            ref = right.at[z, units[u]]
            send(ref, ref, ("g", True, 1, e), z_up)
            send(ref, ref, ("g", False, 1, e), z_dn)
            send(ref, ref, ("f", 0, e), y_mate)

    def spread(up, d, e):
        reach = 4 if (e == 0) == up else 3
        if d > reach:
            return
        panel = ring(z - d if up else z + d, ZS)
        ref = right.at[panel, units[2 + e]]
        arrived(ref, ("g", up, d, e))
        if d < reach:
            send(ref, ref, ("g", up, d + 1, e), z_up if up else z_dn)
        send(ref, ref, ("f", (-d if up else d) % ZS, e), y_mate)

    def left_core():
        send(lown.at[1 - core], lother, ("l", 0), core_mate)

    def left_x():
        arrived(lother, ("l", 0))
        for p in range(PANELS):
            mine = lax.rem(lowner[p], 2) == core
            lpick[p // 2, p % 2] = jnp.where(mine, lown[core, p], lother[p])
        for d in (1, 2, 3):
            to = ring(x + d, XS)
            send(lpick.at[to], lx.at[d - 1], ("lx", d), x_peers[d - 1])

    def left_h():
        for d in (1, 2, 3):
            arrived(lx.at[d - 1], ("lx", d))
        for i in range(2):
            away = ring(x - lowner[2 * x + i] // 8, XS)
            value = lpick[x, i]
            for d in (1, 2, 3):
                value = jnp.where(away == d, lx[d - 1, i], value)
            for j in range(2):
                lhome[2 * i + j] = value[32 * j:32 * (j + 1)]
        for d in (1, 2, 3):
            to = ring(h + d, HS)
            send(lhome.at[to], ly.at[d - 1], ("ly", d), h_peers[d - 1])

    def left_hback():
        for d in (1, 2, 3):
            arrived(ly.at[d - 1], ("ly", d))
        away = ring(h - lax.rem(lowner[2 * x + h // 2] // 2, 4), HS)
        value = lhome[h]
        for d in (1, 2, 3):
            value = jnp.where(away == d, ly[d - 1], value)
        left[core, x, h] = value
        ref = left.at[core, x, h]
        for d in (1, 2, 3):
            send(ref, ref, ("lh", d), h_peers[d - 1])

    def left_xback():
        for d in (1, 2, 3):
            arrived(left.at[core, x, ring(h - d, HS)], ("lh", d))
        ref = left.at[core, x]
        for d in (1, 2, 3):
            send(ref, ref, ("lb", d), x_peers[d - 1])
        send(ref, ref, ("lc", 0), core_mate)

    def left_coreback():
        for d in (1, 2, 3):
            ref = left.at[core, ring(x - d, XS)]
            arrived(ref, ("lb", d))
            send(ref, ref, ("lc", d), core_mate)

    def left_end():
        for d in range(4):
            arrived(left.at[1 - core, ring(x - d, XS)], ("lc", d))

    left_core()
    for tick in range(1, 9):
        if tick == 2:
            left_x()
        if tick == 4:
            left_h()
        if tick == 6:
            left_hback()
        if tick == 8:
            left_xback()
        for u in range(4):
            step = tick - u
            if 1 <= step <= 4:
                collect(u, step)
            elif step == 5:
                home(u)
    for d in (1, 2, 3, 4):
        if d == 3:
            left_coreback()
        for e in (0, 1):
            for up in (True, False):
                spread(up, d, e)
    left_end()
    for e in (0, 1):
        for offset in range(ZS):
            arrived(right.at[ring(z + offset, ZS), 2 * (1 - q) + e], ("f", offset, e))

    slot_row = lax.broadcasted_iota(jnp.int32, (RANK, RANK), 0)
    slot_col = lax.broadcasted_iota(jnp.int32, (RANK, RANK), 1)
    for p in range(PANELS):
        coef = left[1, p // 2, pl.ds(2 * (p % 2), 2)].reshape(RANK, WIDE)
        small = flat_dot(coef, right[p, 0], ((1,), (1,)))
        keep = (slot_row < lrank[p, 0]) & (slot_col < rrank[p, 0])
        small = jnp.where(keep, small * (lscale[p, 0] * rscale[p, 0]), 0.0)
        small_high, small_low = split(small)
        for u in (1, 2, 3):
            wide = right[p, u]
            middle = flat_dot(small_high, wide, ((1,), (0,))) + flat_dot(small_low, wide, ((1,), (0,)))
            high, low = split(middle)
            place = pl.ds(RANK * p, RANK), pl.ds(WIDE * (u - 1), WIDE)
            mid_high[place] = high
            mid_low[place] = low
    basis = left[0].reshape(PANELS * RANK, WIDE)
    out[...] = flat_dot(basis, mid_high[...], ((0,), (0,))) + flat_dot(basis, mid_low[...], ((0,), (0,)))

    for copy in sent:
        copy.wait_send()
    assert len(sent) <= N_SEND and len(slots) <= N_RECV, (len(sent), len(slots))


def shards(
    contribution, left_basis, left_coef, right_coef, right_basis,
    left_rank, left_scale, right_rank, right_scale, left_owner, right_owner,
):
    smem = pl.BlockSpec(memory_space=pltpu.SMEM)
    hbm = pl.BlockSpec(memory_space=pl.ANY)
    unit = (RANK, WIDE)
    update = pl.pallas_call(
        kernel,
        out_shape=jax.ShapeDtypeStruct((ROWS_OUT, COLS_OUT), F32),
        in_specs=[smem] * 6 + [hbm] * 4,
        out_specs=pl.BlockSpec(memory_space=pltpu.VMEM),
        scratch_shapes=[
            pltpu.VMEM((PANELS, 4) + unit, BF16),
            pltpu.VMEM((4, 4) + unit, BF16),
            pltpu.VMEM((4, 4) + unit, BF16),
            pltpu.VMEM((PANELS, 4) + unit, BF16),
            pltpu.VMEM((2,) + unit, BF16),
            pltpu.VMEM((2,) + unit, BF16),
            pltpu.VMEM((2, PANELS) + unit, BF16),
            pltpu.VMEM((PANELS,) + unit, BF16),
            pltpu.VMEM((XS, 2) + unit, BF16),
            pltpu.VMEM((3, 2) + unit, BF16),
            pltpu.VMEM((HS, 32, WIDE), BF16),
            pltpu.VMEM((3, 32, WIDE), BF16),
            pltpu.VMEM((32, WIDE), BF16),
            pltpu.VMEM((2, XS, HS, 32, WIDE), BF16),
            pltpu.VMEM((PANELS * RANK, COLS_OUT), BF16),
            pltpu.VMEM((PANELS * RANK, COLS_OUT), BF16),
            pltpu.SemaphoreType.DMA((6,)),
            pltpu.SemaphoreType.DMA((N_SEND,)),
            pltpu.SemaphoreType.DMA((N_RECV,)),
        ],
        compiler_params=pltpu.CompilerParams(collective_id=0, has_side_effects=True),
    )(
        left_owner, right_owner, left_rank, left_scale, right_rank, right_scale,
        left_basis, left_coef, right_coef, right_basis,
    )
    return contribution - update


def solution(mesh):
    return jax.shard_map(
        shards,
        mesh=mesh,
        in_specs=(
            P("row", "col"),
            P(None, "col", None, "row"),
            P(None, "col", None, "row"),
            P(None, "row", None, "col"),
            P(None, "row", None, "col"),
            P(None, "row"),
            P(None, "row"),
            P(None, "col"),
            P(None, "col"),
            P(),
            P(),
        ),
        out_specs=P("row", "col"),
        check_vma=False,
    )
```

time: 634 us -> 66.6 us (0.11)
  the two profiles are of different devices: /device:TPU:2 before, /device:TPU:4 now
where the time goes in v1:
time: 66.6 us; the launch traced here: 66.3 us
  Pallas kernels  60.8 us (91%)
  local copies, waits for them, and re-layouts  3.36 us (5%)
  other arithmetic  2.1 us (3%)
    pallas_call x1, Pallas kernels, shards(): pl.pallas_call(kernel, out_shape=jax.ShapeDtypeStruct((ROWS_OUT, COLS_OUT...  60.8 us
    unnamed x12, local copies, waits for them, and re-layouts  3.36 us
    sub x1, other arithmetic, shards(): return contribution - update  2.1 us

profile of v1, /device:TPU:4, one launch (start us, length us, event | category | flops | bytes accessed | tf_op | source)
XLA Modules:
  0.0 66.3 jit_solution(13712244528387693198)
XLA Ops:
  0.0 0.0 copy-start.1
  0.0 1.3 %copy.12.lrank = s32[8,1]{1,0:T(8,128)} copy(s32[8,1]{0,1:T(1,128)} %param.16) | data formatting | bytes 64 | tf_op args[5]
  1.3 0.0 copy-done.1
  1.3 0.0 copy-start.2
  1.3 0.7 copy.13.lscale
  2.0 0.0 copy-done.2
  2.0 0.0 copy-start.3
  2.0 0.7 %copy.14.rrank = s32[8,1]{1,0:T(8,128)} copy(s32[8,1]{0,1:T(1,128)S(1)} %copy-done.2) | data formatting | bytes 64 | tf_op args[7]
  2.7 0.0 copy-done.3
  2.7 0.7 %copy.15.rscale = f32[8,1]{1,0:T(8,128)} copy(f32[8,1]{0,1:T(1,128)S(1)} %copy-done.3) | data formatting | bytes 64 | tf_op args[8]
  3.4 0.0 copy-start
  3.4 60.8 %shard_map.109 = f32[256,768]{1,0:T(8,128)} custom-call(s32[8]{0:T(128)} %lowner.1, s32[8]{0:T(128)} %rowner.1, s32[8,1]{1,0:T(8,128)} %copy.12.lrank, f32[8,1]{1,0:T(8,128)} %copy.13.lscale, s32[8,1]{1,0:T(8,128)} %copy.14.rrank, f32[8,1]{1,0:T(8,128)} %copy.15.rscale, bf16[8,1,64,256]{3,2,1,0:T(8,128)(2,1)} %lbasis.1, bf16[8,1,64,256]{3,2,1,0:T(8,128)(2,1)} %lcoef.1, ...), custom_call_target="tpu_custom_call" | custom-call | tf_op jit(solution)/shard_map/pallas_call | solution.py:256
  64.2 0.0 copy-done
  64.2 2.1 %sub.3 = f32[256,768]{1,0:T(8,128)} subtract(f32[256,768]{1,0:T(8,128)S(1)} %copy-done, f32[256,768]{1,0:T(8,128)} %shard_map.109) | non-fusion elementwise | flops 196608 | bytes 2359296 | tf_op jit(solution)/shard_map/sub | solution.py:287
Async XLA Ops:
  0.0 1.3 %copy-start.1 = (f32[8,1]{0,1:T(1,128)S(1)}, f32[8,1]{0,1:T(1,128)}, u32[]{:S(2)}) copy-start(f32[8,1]{0,1:T(1,128)} %param.17) | copy-start | bytes 100
  1.3 0.7 %copy-start.2 = (s32[8,1]{0,1:T(1,128)S(1)}, s32[8,1]{0,1:T(1,128)}, u32[]{:S(2)}) copy-start(s32[8,1]{0,1:T(1,128)} %param.18) | copy-start | bytes 100
  2.0 0.7 %copy-start.3 = (f32[8,1]{0,1:T(1,128)S(1)}, f32[8,1]{0,1:T(1,128)}, u32[]{:S(2)}) copy-start(f32[8,1]{0,1:T(1,128)} %param.19) | copy-start | bytes 100
  3.4 60.8 %copy-start = (f32[256,768]{1,0:T(8,128)S(1)}, f32[256,768]{1,0:T(8,128)}, u32[]{:S(2)}) copy-start(f32[256,768]{1,0:T(8,128)} %param.11) | copy-start | bytes 2359300

commit v2 on v1

v2 whole, which is shorter than its diff:
```python
import jax
import jax.numpy as jnp
from jax import lax
from jax.experimental import pallas as pl
from jax.experimental.pallas import tpu as pltpu
from jax.sharding import PartitionSpec as P

MESH = pl.DeviceIdType.MESH
BF16, F32 = jnp.bfloat16, jnp.float32
PANELS, RANK, WIDE = 8, 64, 256
ROWS_OUT, COLS_OUT = 256, 768
ZS, XS, HS = 8, 4, 4
FAR_FIRST = (4, 3, 5, 2, 6, 1, 7)
NEAR, FAR = (0, 1, 7, 2, 6), (3, 5, 4)


def ring(value, size):
    return lax.rem(value + 4 * size, size)


def flat_dot(left, right, dims):
    return lax.dot_general(left, right, (dims, ((), ())), preferred_element_type=F32)


def split(value):
    high = value.astype(BF16)
    return high, (value - high.astype(F32)).astype(BF16)


def kernel(
    lowner, rowner, lrank, lscale, rrank, rscale,
    lbasis, lcoef, rcoef, rbasis,
    out,
    own, yin, zout, zin, right,
    lown, lother, lpick, lx, lhome, ly, left,
    basis, mid_high, mid_low,
    load_sem, send_sem, y_sem, z_sem, g_sem, f_sem, l_sem,
):
    row, col = lax.axis_index("row"), lax.axis_index("col")
    z, q = row // 2, lax.rem(row, 2)
    x, h, core = col // 8, lax.rem(col // 2, 4), lax.rem(col, 2)

    def at_z(offset):
        return (ring(z + offset, ZS) * 2 + q, col)

    def at_col(xx, hh, cc):
        return (row, (xx * 4 + hh) * 2 + cc)

    y_mate, core_mate = (z * 2 + 1 - q, col), at_col(x, h, 1 - core)
    x_peers = [at_col(ring(x + d, XS), h, core) for d in (1, 2, 3)]
    h_peers = [at_col(x, ring(h + d, HS), core) for d in (1, 2, 3)]
    everyone = [at_z(o) for o in FAR_FIRST] + [y_mate, core_mate] + x_peers + h_peers

    loads = [
        pltpu.make_async_copy(rcoef.at[:, 0], own.at[:, 0], load_sem.at[0]),
        pltpu.make_async_copy(lbasis.at[:, 0], lown.at[0], load_sem.at[4]),
        pltpu.make_async_copy(lcoef.at[:, 0], lown.at[1], load_sem.at[5]),
    ] + [
        pltpu.make_async_copy(
            rbasis.at[:, 0, :, pl.ds(WIDE * (u - 1), WIDE)], own.at[:, u], load_sem.at[u]
        )
        for u in (1, 2, 3)
    ]
    for load in loads:
        load.start()

    barrier = pltpu.get_barrier_semaphore()
    for peer in everyone:
        pl.semaphore_signal(barrier, inc=1, device_id=peer, device_id_type=MESH)
    for load in loads:
        load.wait()
    pl.semaphore_wait(barrier, len(everyone))

    def send(src, dst, sem, peer, group):
        pltpu.make_async_remote_copy(
            src_ref=src, dst_ref=dst, send_sem=send_sem.at[group],
            recv_sem=sem, device_id=peer, device_id_type=MESH,
        ).start()

    def wait(ref, sem):
        pltpu.make_async_remote_copy(
            src_ref=ref, dst_ref=ref, send_sem=send_sem.at[0],
            recv_sem=sem, device_id=core_mate, device_id_type=MESH,
        ).wait_recv()

    def wait_sent(ref, group):
        pltpu.make_async_remote_copy(
            src_ref=ref, dst_ref=ref, send_sem=send_sem.at[group],
            recv_sem=z_sem, device_id=core_mate, device_id_type=MESH,
        ).wait_send()

    stay, leave = pl.ds(2 * q, 2), pl.ds(2 * (1 - q), 2)

    def left_core():
        send(lown.at[1 - core], lother, l_sem.at[0], core_mate, 1)

    def left_x():
        wait(lother, l_sem.at[0])
        for p in range(PANELS):
            mine = lax.rem(lowner[p], 2) == core
            lpick[p // 2, p % 2] = jnp.where(mine, lown[core, p], lother[p])
        for d in (2, 1, 3):
            send(lpick.at[ring(x + d, XS)], lx.at[d - 1], l_sem.at[1], x_peers[d - 1], 2)

    def left_h():
        wait(lx, l_sem.at[1])
        for i in range(2):
            away = ring(x - lowner[2 * x + i] // 8, XS)
            value = lpick[x, i]
            for d in (1, 2, 3):
                value = jnp.where(away == d, lx[d - 1, i], value)
            for j in range(2):
                lhome[2 * i + j] = value[32 * j:32 * (j + 1)]
        for d in (2, 1, 3):
            send(lhome.at[ring(h + d, HS)], ly.at[d - 1], l_sem.at[2], h_peers[d - 1], 3)

    def left_hback():
        wait(ly, l_sem.at[2])
        away = ring(h - lax.rem(lowner[2 * x + h // 2] // 2, 4), HS)
        value = lhome[h]
        for d in (1, 2, 3):
            value = jnp.where(away == d, ly[d - 1], value)
        left[core, x, h] = value
        ref = left.at[core, x, h]
        for d in (2, 1, 3):
            send(ref, ref, l_sem.at[3], h_peers[d - 1], 4)

    def left_xback():
        wait(ly, l_sem.at[3])
        ref = left.at[core, x]
        for d in (2, 1, 3):
            send(ref, ref, l_sem.at[3 + d], x_peers[d - 1], 5)
        send(ref, ref, l_sem.at[7], core_mate, 6)

    def left_coreback():
        for d in (1, 3, 2):
            ref = left.at[core, ring(x - d, XS)]
            wait(ref, l_sem.at[3 + d])
            send(ref, ref, l_sem.at[7], core_mate, 6)

    def left_end():
        wait(lown.at[0], l_sem.at[7])

    def pick(offset):
        panel = ring(z + offset, ZS)
        wait(yin.at[offset], y_sem.at[offset])
        mine = lax.rem(rowner[panel], 2) == q
        return jnp.where(mine, own[panel, stay], yin[offset])

    def scatter(offset):
        zout[offset - 1] = pick(offset)
        send(zout.at[offset - 1], zin.at[offset], z_sem, at_z(offset), 7)

    def mine_at(offset):
        return right.at[ring(z + offset, ZS), stay]

    def forward(offset):
        send(mine_at(offset), mine_at(offset), f_sem.at[int(offset in FAR)], y_mate, 8)

    def received(offset):
        wait(mine_at(offset), g_sem.at[offset])

    left_core()
    for o in FAR_FIRST + (0,):
        send(own.at[ring(z + o, ZS), leave], yin.at[o], y_sem.at[o], y_mate, 0)
    left_x()
    for o in FAR_FIRST[:4]:
        scatter(o)
    left_h()
    for o in FAR_FIRST[4:]:
        scatter(o)
    zin[0] = pick(0)
    left_hback()
    wait(zin.at[pl.ds(1, 7)], z_sem)
    right[z, stay] = zin[ring(z - rowner[z] // 2, ZS)]
    home = mine_at(0)
    for d in (2, -2, 1, -1):
        send(home, home, g_sem.at[-d % ZS], at_z(d), 9)
    forward(0)
    left_xback()
    for d in (2, -2):
        received(-d % ZS)
        ref = mine_at(-d)
        e = 0 if d > 0 else 1
        one = right.at[ring(z - d, ZS), 2 * q + e]
        send(one, one, g_sem.at[4], at_z(d), 11)
        send(ref, ref, g_sem.at[(-d - d // 2) % ZS], at_z(d // 2), 10)
        forward(-d % ZS)
    for o in (1, 7):
        received(o)
        forward(o)
    left_coreback()
    for o in FAR:
        received(o)
        forward(o)
    left_end()

    slot_row = lax.broadcasted_iota(jnp.int32, (RANK, RANK), 0)
    slot_col = lax.broadcasted_iota(jnp.int32, (RANK, RANK), 1)

    def products(offsets, start):
        for i, o in enumerate(offsets):
            p = ring(z + o, ZS)
            pair = p // 2, pl.ds(2 * lax.rem(p, 2), 2)
            rows = pl.ds(RANK * (start + i), RANK)
            basis[rows, :] = left[(0,) + pair].reshape(RANK, WIDE)
            coef = left[(1,) + pair].reshape(RANK, WIDE)
            small = flat_dot(coef, right[p, 0], ((1,), (1,)))
            keep = (slot_row < lrank[0, p]) & (slot_col < rrank[0, p])
            small = jnp.where(keep, small * (lscale[0, p] * rscale[0, p]), 0.0)
            small_high, small_low = split(small)
            for u in (1, 2, 3):
                wide = right[p, u]
                middle = flat_dot(small_high, wide, ((1,), (0,))) + flat_dot(small_low, wide, ((1,), (0,)))
                high, low = split(middle)
                place = rows, pl.ds(WIDE * (u - 1), WIDE)
                mid_high[place] = high
                mid_low[place] = low
        rows = pl.ds(RANK * start, RANK * len(offsets))
        lhs = basis[rows, :]
        return flat_dot(lhs, mid_high[rows, :], ((0,), (0,))) + flat_dot(lhs, mid_low[rows, :], ((0,), (0,)))

    wait(zin.at[pl.ds(0, 5)], f_sem.at[0])
    out[...] = products(NEAR, 0)
    wait(zin.at[pl.ds(0, 3)], f_sem.at[1])
    out[...] += products(FAR, len(NEAR))

    wait_sent(lown.at[0], 1)
    wait_sent(lx, 2)
    wait_sent(ly, 3)
    wait_sent(ly, 4)
    wait_sent(lx, 5)
    wait_sent(lown.at[0], 6)
    wait_sent(zin, 0)
    wait_sent(zout, 7)
    wait_sent(zin, 8)
    wait_sent(zin.at[pl.ds(0, 4)], 9)
    wait_sent(zin.at[pl.ds(0, 2)], 10)
    wait_sent(zin.at[0], 11)


def shards(
    contribution, left_basis, left_coef, right_coef, right_basis,
    left_rank, left_scale, right_rank, right_scale, left_owner, right_owner,
):
    smem = pl.BlockSpec(memory_space=pltpu.SMEM)
    hbm = pl.BlockSpec(memory_space=pl.ANY)
    unit = (RANK, WIDE)
    update = pl.pallas_call(
        kernel,
        out_shape=jax.ShapeDtypeStruct((ROWS_OUT, COLS_OUT), F32),
        in_specs=[smem] * 6 + [hbm] * 4,
        out_specs=pl.BlockSpec(memory_space=pltpu.VMEM),
        scratch_shapes=[
            pltpu.VMEM((PANELS, 4) + unit, BF16),
            pltpu.VMEM((ZS, 2) + unit, BF16),
            pltpu.VMEM((ZS - 1, 2) + unit, BF16),
            pltpu.VMEM((ZS, 2) + unit, BF16),
            pltpu.VMEM((PANELS, 4) + unit, BF16),
            pltpu.VMEM((2, PANELS) + unit, BF16),
            pltpu.VMEM((PANELS,) + unit, BF16),
            pltpu.VMEM((XS, 2) + unit, BF16),
            pltpu.VMEM((3, 2) + unit, BF16),
            pltpu.VMEM((HS, 32, WIDE), BF16),
            pltpu.VMEM((3, 32, WIDE), BF16),
            pltpu.VMEM((2, XS, HS, 32, WIDE), BF16),
            pltpu.VMEM((PANELS * RANK, WIDE), BF16),
            pltpu.VMEM((PANELS * RANK, COLS_OUT), BF16),
            pltpu.VMEM((PANELS * RANK, COLS_OUT), BF16),
            pltpu.SemaphoreType.DMA((6,)),
            pltpu.SemaphoreType.DMA((12,)),
            pltpu.SemaphoreType.DMA((ZS,)),
            pltpu.SemaphoreType.DMA,
            pltpu.SemaphoreType.DMA((ZS,)),
            pltpu.SemaphoreType.DMA((2,)),
            pltpu.SemaphoreType.DMA((8,)),
        ],
        compiler_params=pltpu.CompilerParams(collective_id=0, has_side_effects=True),
    )(
        left_owner, right_owner, left_rank.T, left_scale.T, right_rank.T, right_scale.T,
        left_basis, left_coef, right_coef, right_basis,
    )
    return contribution - update


def solution(mesh):
    return jax.shard_map(
        shards,
        mesh=mesh,
        in_specs=(
            P("row", "col"),
            P(None, "col", None, "row"),
            P(None, "col", None, "row"),
            P(None, "row", None, "col"),
            P(None, "row", None, "col"),
            P(None, "row"),
            P(None, "row"),
            P(None, "col"),
            P(None, "col"),
            P(),
            P(),
        ),
        out_specs=P("row", "col"),
        check_vma=False,
    )
```

time: 66.6 us -> 50.4 us (0.76)
  Pallas kernels: 60.8 us -> 48.1 us
  local copies, waits for them, and re-layouts: 3.36 us -> 0.01 us
    pallas_call x1, Pallas kernels: 60.8 us -> 48.1 us  [shards(): pl.pallas_call(kernel, out_shape=jax.ShapeDtypeStruct((ROWS_OUT, COLS_OUT...]
    unnamed x12 -> x2, local copies, waits for them, and re-layouts: 3.36 us -> 0.01 us
where the time goes in v2:
time: 50.4 us; the launch traced here: 50.2 us
  Pallas kernels  48.1 us (95%)
  other arithmetic  2.1 us (4%)
    pallas_call x1, Pallas kernels, shards(): pl.pallas_call(kernel, out_shape=jax.ShapeDtypeStruct((ROWS_OUT, COLS_OUT...  48.1 us
    sub x1, other arithmetic, shards(): return contribution - update  2.1 us

profile of v2, /device:TPU:4, one launch (start us, length us, event | category | flops | bytes accessed | tf_op | source)
XLA Modules:
  0.0 50.2 jit_solution(4692487435849883484)
XLA Ops:
  0.0 0.0 copy-start
  0.0 48.1 %shard_map.109 = f32[256,768]{1,0:T(8,128)} custom-call(s32[8]{0:T(128)} %lowner.1, s32[8]{0:T(128)} %rowner.1, s32[1,8]{1,0:T(1,128)} %bitcast.4, f32[1,8]{1,0:T(1,128)} %bitcast.5, s32[1,8]{1,0:T(1,128)} %bitcast.6, f32[1,8]{1,0:T(1,128)} %bitcast.7, bf16[8,1,64,256]{3,2,1,0:T(8,128)(2,1)} %lbasis.1, bf16[8,1,64,256]{3,2,1,0:T(8,128)(2,1)} %lcoef.1, ...), custom_call_target="tpu_custom_call" | custom-call | tf_op jit(solution)/shard_map/pallas_call | solution.py:249
  48.1 0.0 copy-done
  48.1 2.1 %sub.3 = f32[256,768]{1,0:T(8,128)} subtract(f32[256,768]{1,0:T(8,128)S(1)} %copy-done, f32[256,768]{1,0:T(8,128)} %shard_map.109) | non-fusion elementwise | flops 196608 | bytes 2359296 | tf_op jit(solution)/shard_map/sub | solution.py:283
Async XLA Ops:
  0.0 48.1 %copy-start = (f32[256,768]{1,0:T(8,128)S(1)}, f32[256,768]{1,0:T(8,128)}, u32[]{:S(2)}) copy-start(f32[256,768]{1,0:T(8,128)} %param.11) | copy-start | bytes 2359300

commit v3 on v2

--- a/solution.py
+++ b/solution.py
@@ -11,7 +11,8 @@
 ROWS_OUT, COLS_OUT = 256, 768
 ZS, XS, HS = 8, 4, 4
 FAR_FIRST = (4, 3, 5, 2, 6, 1, 7)
-NEAR, FAR = (0, 1, 7, 2, 6), (3, 5, 4)
+NEAR, FAR = (0, 1, 7, 2, 6), (3, 5)
+F_SLOT = {0: 0, 1: 1, 2: 1, 6: 1, 3: 2, 5: 2, 4: 3}
 
 
 def ring(value, size):
@@ -141,58 +142,75 @@
     def left_end():
         wait(lown.at[0], l_sem.at[7])
 
-    def pick(offset):
+    def keep_at(offset, e):
+        return right.at[ring(z + offset, ZS), 2 * q + e]
+
+    def scatter(offset):
         panel = ring(z + offset, ZS)
-        wait(yin.at[offset], y_sem.at[offset])
         mine = lax.rem(rowner[panel], 2) == q
-        return jnp.where(mine, own[panel, stay], yin[offset])
-
-    def scatter(offset):
-        zout[offset - 1] = pick(offset)
-        send(zout.at[offset - 1], zin.at[offset], z_sem, at_z(offset), 7)
-
-    def mine_at(offset):
-        return right.at[ring(z + offset, ZS), stay]
-
-    def forward(offset):
-        send(mine_at(offset), mine_at(offset), f_sem.at[int(offset in FAR)], y_mate, 8)
-
-    def received(offset):
-        wait(mine_at(offset), g_sem.at[offset])
+        for e in (0, 1):
+            wait(yin.at[offset, e], y_sem.at[offset, e])
+            value = jnp.where(mine, own[panel, 2 * q + e], yin[offset, e])
+            if offset:
+                zout[offset - 1, e] = value
+                send(zout.at[offset - 1, e], zin.at[offset, e], z_sem, at_z(offset), 7)
+            else:
+                zin[0, e] = value
+
+    def relay(offset, e, to):
+        ref = keep_at(offset, e)
+        send(ref, ref, g_sem.at[(offset - to) % ZS, e], at_z(to), 9)
+
+    def forward(offset, e):
+        ref = keep_at(offset, e)
+        send(ref, ref, f_sem.at[F_SLOT[offset]], y_mate, 8)
+
+    def received(offset, e):
+        wait(keep_at(offset, e), g_sem.at[offset, e])
 
     left_core()
     for o in FAR_FIRST + (0,):
-        send(own.at[ring(z + o, ZS), leave], yin.at[o], y_sem.at[o], y_mate, 0)
+        for e in (0, 1):
+            send(own.at[ring(z + o, ZS), 2 * (1 - q) + e], yin.at[o, e], y_sem.at[o, e], y_mate, 0)
     left_x()
     for o in FAR_FIRST[:4]:
         scatter(o)
     left_h()
-    for o in FAR_FIRST[4:]:
+    for o in FAR_FIRST[4:] + (0,):
         scatter(o)
-    zin[0] = pick(0)
     left_hback()
     wait(zin.at[pl.ds(1, 7)], z_sem)
     right[z, stay] = zin[ring(z - rowner[z] // 2, ZS)]
-    home = mine_at(0)
-    for d in (2, -2, 1, -1):
-        send(home, home, g_sem.at[-d % ZS], at_z(d), 9)
-    forward(0)
+    for e in (0, 1):
+        forward(0, e)
+        relay(0, e, 2)
+        relay(0, 1 - e, -2)
+    for e in (0, 1):
+        relay(0, e, 1)
+        relay(0, 1 - e, -1)
+    other = right.at[z, leave]
+    wait(other, f_sem.at[F_SLOT[0]])
+    for d in (1, -1):
+        send(other, other, f_sem.at[F_SLOT[1]], at_z(d), 10)
     left_xback()
-    for d in (2, -2):
-        received(-d % ZS)
-        ref = mine_at(-d)
-        e = 0 if d > 0 else 1
-        one = right.at[ring(z - d, ZS), 2 * q + e]
-        send(one, one, g_sem.at[4], at_z(d), 11)
-        send(ref, ref, g_sem.at[(-d - d // 2) % ZS], at_z(d // 2), 10)
-        forward(-d % ZS)
-    for o in (1, 7):
-        received(o)
-        forward(o)
+    for turn in (0, 1):
+        for o, step, e in ((6, 1, turn), (2, -1, 1 - turn)):
+            received(o, e)
+            if turn == 0:
+                relay(o, e, 2 * step)
+            relay(o, e, step)
+            forward(o, e)
     left_coreback()
-    for o in FAR:
-        received(o)
-        forward(o)
+    for e in (0, 1):
+        for o in (7, 1):
+            received(o, e)
+    for turn in (0, 1):
+        for o, e in ((5, turn), (3, 1 - turn)):
+            received(o, e)
+            forward(o, e)
+    for e in (0, 1):
+        received(4, e)
+        forward(4, e)
     left_end()
 
     slot_row = lax.broadcasted_iota(jnp.int32, (RANK, RANK), 0)
@@ -220,10 +238,12 @@
         lhs = basis[rows, :]
         return flat_dot(lhs, mid_high[rows, :], ((0,), (0,))) + flat_dot(lhs, mid_low[rows, :], ((0,), (0,)))
 
-    wait(zin.at[pl.ds(0, 5)], f_sem.at[0])
+    wait(zin.at[pl.ds(0, 4)], f_sem.at[F_SLOT[1]])
     out[...] = products(NEAR, 0)
-    wait(zin.at[pl.ds(0, 3)], f_sem.at[1])
+    wait(zin.at[pl.ds(0, 2)], f_sem.at[F_SLOT[3]])
     out[...] += products(FAR, len(NEAR))
+    wait(zin.at[0], f_sem.at[F_SLOT[4]])
+    out[...] += products((4,), len(NEAR) + len(FAR))
 
     wait_sent(lown.at[0], 1)
     wait_sent(lx, 2)
@@ -233,10 +253,9 @@
     wait_sent(lown.at[0], 6)
     wait_sent(zin, 0)
     wait_sent(zout, 7)
-    wait_sent(zin, 8)
-    wait_sent(zin.at[pl.ds(0, 4)], 9)
+    wait_sent(zin.at[pl.ds(0, 6)], 8)
+    wait_sent(zout, 9)
     wait_sent(zin.at[pl.ds(0, 2)], 10)
-    wait_sent(zin.at[0], 11)
 
 
 def shards(
@@ -248,7 +267,7 @@
     unit = (RANK, WIDE)
     update = pl.pallas_call(
         kernel,
-        out_shape=jax.ShapeDtypeStruct((ROWS_OUT, COLS_OUT), F32),
+        out_shape=pltpu.VMEM((ROWS_OUT, COLS_OUT), F32),
         in_specs=[smem] * 6 + [hbm] * 4,
         out_specs=pl.BlockSpec(memory_space=pltpu.VMEM),
         scratch_shapes=[
@@ -268,11 +287,11 @@
             pltpu.VMEM((PANELS * RANK, COLS_OUT), BF16),
             pltpu.VMEM((PANELS * RANK, COLS_OUT), BF16),
             pltpu.SemaphoreType.DMA((6,)),
-            pltpu.SemaphoreType.DMA((12,)),
-            pltpu.SemaphoreType.DMA((ZS,)),
+            pltpu.SemaphoreType.DMA((11,)),
+            pltpu.SemaphoreType.DMA((ZS, 2)),
             pltpu.SemaphoreType.DMA,
-            pltpu.SemaphoreType.DMA((ZS,)),
-            pltpu.SemaphoreType.DMA((2,)),
+            pltpu.SemaphoreType.DMA((ZS, 2)),
+            pltpu.SemaphoreType.DMA((4,)),
             pltpu.SemaphoreType.DMA((8,)),
         ],
         compiler_params=pltpu.CompilerParams(collective_id=0, has_side_effects=True),

time: 50.4 us -> 46.4 us (0.921)
  the two profiles are of different devices: /device:TPU:4 before, /device:TPU:14 now
where the time goes in v3:
time: 46.4 us; the launch traced here: 46.3 us
  Pallas kernels  45.3 us (98%)
  other arithmetic  0.97 us (2%)
    pallas_call x1, Pallas kernels, shards(): pl.pallas_call(kernel, out_shape=pltpu.VMEM((ROWS_OUT, COLS_OUT), F32), i...  45.3 us
    sub x1, other arithmetic, shards(): return contribution - update  0.97 us

profile of v3, /device:TPU:14, one launch (start us, length us, event | category | flops | bytes accessed | tf_op | source)
XLA Modules:
  0.0 46.3 jit_solution(18342777189538182395)
XLA Ops:
  0.0 0.0 copy-start
  0.0 45.3 %shard_map.109 = f32[256,768]{1,0:T(8,128)S(1)} custom-call(s32[8]{0:T(128)} %lowner.1, s32[8]{0:T(128)} %rowner.1, s32[1,8]{1,0:T(1,128)} %bitcast.4, f32[1,8]{1,0:T(1,128)} %bitcast.5, s32[1,8]{1,0:T(1,128)} %bitcast.6, f32[1,8]{1,0:T(1,128)} %bitcast.7, bf16[8,1,64,256]{3,2,1,0:T(8,128)(2,1)} %lbasis.1, bf16[8,1,64,256]{3,2,1,0:T(8,128)(2,1)} %lcoef.1, ...), custom_call_target="tpu_custom_call" | custom-call | tf_op jit(solution)/shard_map/pallas_call | solution.py:268
  45.3 0.0 copy-done
  45.3 1.0 %sub.3 = f32[256,768]{1,0:T(8,128)} subtract(f32[256,768]{1,0:T(8,128)S(1)} %copy-done, f32[256,768]{1,0:T(8,128)S(1)} %shard_map.109) | non-fusion elementwise | flops 196608 | bytes 2359296 | tf_op jit(solution)/shard_map/sub | solution.py:302
Async XLA Ops:
  0.0 45.3 %copy-start = (f32[256,768]{1,0:T(8,128)S(1)}, f32[256,768]{1,0:T(8,128)}, u32[]{:S(2)}) copy-start(f32[256,768]{1,0:T(8,128)} %param.11) | copy-start | bytes 2359300

commit v4 on v3

v4 whole, which is shorter than its diff:
```python
import jax
import jax.numpy as jnp
from jax import lax
from jax.experimental import pallas as pl
from jax.experimental.pallas import tpu as pltpu
from jax.sharding import PartitionSpec as P

MESH = pl.DeviceIdType.MESH
BF16, F32 = jnp.bfloat16, jnp.float32
PANELS, RANK, WIDE = 8, 64, 256
ROWS_OUT, COLS_OUT = 256, 768
ZS, XS, HS = 8, 4, 4
FAR_FIRST = (4, 3, 5, 2, 6)
NEAR, FAR = (0, 1, 7, 2, 6), (3, 5)
F_SLOT = {0: 0, 1: 1, 2: 1, 6: 1, 3: 2, 5: 2, 4: 3}
G_SLOT = {(6, 0): 0, (6, 1): 1, (2, 0): 2, (2, 1): 3, (5, 0): 5, (5, 1): 6, (3, 0): 7, (3, 1): 8}
SENT = 91


def ring(value, size):
    return lax.rem(value + 4 * size, size)


def flat_dot(left, right, dims):
    return lax.dot_general(left, right, (dims, ((), ())), preferred_element_type=F32)


def split(value):
    high = value.astype(BF16)
    return high, (value - high.astype(F32)).astype(BF16)


def kernel(
    lowner, rowner, lrank, lscale, rrank, rscale,
    lbasis, lcoef, rcoef, rbasis,
    out,
    own, yin, zout, passed, zin, near, hout, hin, right,
    lown, lother, lpick, lx, lhome, ly, left,
    basis, mid_high, mid_low, all_sent,
    load_sem, send_sem, y_sem, p_sem, z_sem, n_sem, g_sem, f_sem, l_sem,
):
    row, col = lax.axis_index("row"), lax.axis_index("col")
    z, q = row // 2, lax.rem(row, 2)
    x, h, core = col // 8, lax.rem(col // 2, 4), lax.rem(col, 2)

    def at_z(offset):
        return (ring(z + offset, ZS) * 2 + q, col)

    def at_col(xx, hh, cc):
        return (row, (xx * 4 + hh) * 2 + cc)

    y_mate, core_mate = (z * 2 + 1 - q, col), at_col(x, h, 1 - core)
    x_peers = [at_col(ring(x + d, XS), h, core) for d in (1, 2, 3)]
    h_peers = [at_col(x, ring(h + d, HS), core) for d in (1, 2, 3)]
    everyone = [at_z(o) for o in FAR_FIRST + (1, 7)] + [y_mate, core_mate] + x_peers + h_peers

    for u in (1, 2, 3):
        columns = pl.ds(WIDE * (u - 1), WIDE)
        pltpu.make_async_copy(rbasis.at[:, 0, :, columns], own.at[:, u], load_sem.at[0]).start()
    pltpu.make_async_copy(rcoef.at[:, 0], own.at[:, 0], load_sem.at[0]).start()
    pltpu.make_async_copy(lbasis.at[:, 0], lown.at[0], load_sem.at[1]).start()
    pltpu.make_async_copy(lcoef.at[:, 0], lown.at[1], load_sem.at[1]).start()

    barrier = pltpu.get_barrier_semaphore()
    for peer in everyone:
        pl.semaphore_signal(barrier, inc=1, device_id=peer, device_id_type=MESH)

    def send(src, dst, sem, peer):
        pltpu.make_async_remote_copy(
            src_ref=src, dst_ref=dst, send_sem=send_sem,
            recv_sem=sem, device_id=peer, device_id_type=MESH,
        ).start()

    def wait(ref, sem):
        pltpu.make_async_remote_copy(
            src_ref=ref, dst_ref=ref, send_sem=send_sem,
            recv_sem=sem, device_id=core_mate, device_id_type=MESH,
        ).wait_recv()

    stay, leave = pl.ds(2 * q, 2), pl.ds(2 * (1 - q), 2)

    def left_core():
        send(lown.at[1 - core], lother, l_sem.at[0], core_mate)

    def left_x():
        wait(lother, l_sem.at[0])
        for p in range(PANELS):
            mine = lax.rem(lowner[p], 2) == core
            lpick[p // 2, p % 2] = jnp.where(mine, lown[core, p], lother[p])
        for d in (2, 1, 3):
            send(lpick.at[ring(x + d, XS)], lx.at[d - 1], l_sem.at[1], x_peers[d - 1])

    def left_h():
        wait(lx, l_sem.at[1])
        for i in range(2):
            away = ring(x - lowner[2 * x + i] // 8, XS)
            value = lpick[x, i]
            for d in (1, 2, 3):
                value = jnp.where(away == d, lx[d - 1, i], value)
            for j in range(2):
                lhome[2 * i + j] = value[32 * j:32 * (j + 1)]
        for d in (2, 1, 3):
            send(lhome.at[ring(h + d, HS)], ly.at[d - 1], l_sem.at[2], h_peers[d - 1])

    def left_hback():
        wait(ly, l_sem.at[2])
        away = ring(h - lax.rem(lowner[2 * x + h // 2] // 2, 4), HS)
        value = lhome[h]
        for d in (1, 2, 3):
            value = jnp.where(away == d, ly[d - 1], value)
        left[core, x, h] = value
        ref = left.at[core, x, h]
        for d in (2, 1, 3):
            send(ref, ref, l_sem.at[3], h_peers[d - 1])

    def left_xback():
        wait(ly, l_sem.at[3])
        ref = left.at[core, x]
        for d in (2, 1, 3):
            send(ref, ref, l_sem.at[4], x_peers[d - 1])
        send(ref, ref, l_sem.at[5], core_mate)

    def left_coreback():
        wait(lx, l_sem.at[4])
        for d in (1, 3, 2):
            ref = left.at[core, ring(x - d, XS)]
            send(ref, ref, l_sem.at[5], core_mate)

    def left_end():
        wait(lown.at[0], l_sem.at[5])

    def keep_at(offset, e):
        return right.at[ring(z + offset, ZS), 2 * q + e]

    def paired(offset):
        panel, slot = ring(z + offset, ZS), FAR_FIRST.index(offset)
        wait(yin.at[slot], y_sem.at[slot])
        mine = lax.rem(rowner[panel], 2) == q
        return jnp.where(mine, own[panel, stay], yin[slot])

    def begin(offset):
        slot = FAR_FIRST.index(offset)
        zout[slot] = paired(offset)
        if offset == 4:
            for e, to in ((0, 2), (1, -2)):
                send(zout.at[slot, e], passed.at[e, 2], p_sem.at[e], at_z(to))
        else:
            way, to = (0, 1) if offset == 3 else (1, -1)
            send(zout.at[slot], passed.at[way, pl.ds(0, 2)], p_sem.at[way], at_z(to))

    def merge(way):
        offset = (2, 6)[way]
        slot = FAR_FIRST.index(offset)
        panel = ring(z + offset, ZS)
        value = paired(offset)
        wait(passed.at[way], p_sem.at[way])
        away = ring(panel - rowner[panel] // 2, ZS)
        value = jnp.where(away == (3, 5)[way], passed[way, 0:2], value)
        zout[slot] = value
        zout[slot, way] = jnp.where(away == 4, passed[way, 2], value[way])
        for e in (way, 1 - way):
            send(zout.at[slot, e], zin.at[way, e], z_sem, at_z((2, -2)[way]))

    source = ring(z - rowner[z] // 2, ZS)

    def near_pick(units):
        value = jnp.where(source == 1, near[0, units], own[z, units])
        return jnp.where(source == 7, near[1, units], value)

    def relay(offset, e, to):
        ref = keep_at(offset, e)
        there = (offset - to) % ZS
        slot = 4 if there in (1, 7) else 9 if there == 4 else G_SLOT[there, e]
        send(ref, ref, g_sem.at[slot], at_z(to))

    def forward(offset, e):
        ref = keep_at(offset, e)
        send(ref, ref, f_sem.at[F_SLOT[offset]], y_mate)

    def received(offset, e):
        wait(keep_at(offset, e), g_sem.at[G_SLOT[offset, e]])

    wait(own, load_sem.at[0])
    pl.semaphore_wait(barrier, len(everyone))
    for slot, o in enumerate(FAR_FIRST):
        send(own.at[ring(z + o, ZS), leave], yin.at[slot], y_sem.at[slot], y_mate)
    for i, d in enumerate((1, -1)):
        panel = ring(z + d, ZS)
        for units in (leave, stay):
            send(own.at[panel, units], near.at[i, units], n_sem.at[0], at_z(d))
    wait(lown, load_sem.at[1])
    left_core()
    left_x()
    for o in FAR_FIRST[:3]:
        begin(o)
    wait(near, n_sem.at[0])
    hout[...] = near_pick(leave)
    send(hout, hin, n_sem.at[1], y_mate)
    left_h()
    merge(0)
    merge(1)
    wait(hin, n_sem.at[1])
    close = jnp.where(lax.rem(rowner[z], 2) == q, near_pick(stay), hin[...])
    left_hback()
    wait(zin, z_sem)
    for e in (0, 1):
        below = (source == 2) | (source == 3) | ((source == 4) & (e == 0))
        above = (source == 5) | (source == 6) | ((source == 4) & (e == 1))
        value = jnp.where(below, zin[0, e], jnp.where(above, zin[1, e], close[e]))
        right[z, 2 * q + e] = value
    for e in (0, 1):
        forward(0, e)
        relay(0, e, 2)
        relay(0, 1 - e, -2)
    for e in (0, 1):
        relay(0, e, 1)
        relay(0, 1 - e, -1)
    left_xback()
    for turn in (0, 1):
        for o, step, e in ((6, 1, turn), (2, -1, 1 - turn)):
            received(o, e)
            if turn == 0:
                relay(o, e, 2 * step)
            relay(o, e, step)
            forward(o, e)
    other = right.at[z, leave]
    wait(other, f_sem.at[F_SLOT[0]])
    for d in (1, -1):
        send(other, other, f_sem.at[F_SLOT[1]], at_z(d))
    left_coreback()
    for turn in (0, 1):
        for o, e in ((5, turn), (3, 1 - turn)):
            received(o, e)
            forward(o, e)
    wait(hin, g_sem.at[9])
    for e in (0, 1):
        forward(4, e)
    wait(own.at[0], g_sem.at[4])
    left_end()

    slot_row = lax.broadcasted_iota(jnp.int32, (RANK, RANK), 0)
    slot_col = lax.broadcasted_iota(jnp.int32, (RANK, RANK), 1)

    def products(offsets, start):
        for i, o in enumerate(offsets):
            p = ring(z + o, ZS)
            pair = p // 2, pl.ds(2 * lax.rem(p, 2), 2)
            rows = pl.ds(RANK * (start + i), RANK)
            basis[rows, :] = left[(0,) + pair].reshape(RANK, WIDE)
            coef = left[(1,) + pair].reshape(RANK, WIDE)
            small = flat_dot(coef, right[p, 0], ((1,), (1,)))
            keep = (slot_row < lrank[0, p]) & (slot_col < rrank[0, p])
            small = jnp.where(keep, small * (lscale[0, p] * rscale[0, p]), 0.0)
            small_high, small_low = split(small)
            for u in (1, 2, 3):
                wide = right[p, u]
                middle = flat_dot(small_high, wide, ((1,), (0,))) + flat_dot(small_low, wide, ((1,), (0,)))
                high, low = split(middle)
                place = rows, pl.ds(WIDE * (u - 1), WIDE)
                mid_high[place] = high
                mid_low[place] = low
        rows = pl.ds(RANK * start, RANK * len(offsets))
        lhs = basis[rows, :]
        return flat_dot(lhs, mid_high[rows, :], ((0,), (0,))) + flat_dot(lhs, mid_low[rows, :], ((0,), (0,)))

    wait(own.at[pl.ds(0, 2)], f_sem.at[F_SLOT[1]])
    out[...] = products(NEAR, 0)
    wait(own.at[0], f_sem.at[F_SLOT[3]])
    out[...] += products(FAR, len(NEAR))
    wait(hin, f_sem.at[F_SLOT[4]])
    out[...] += products((4,), len(NEAR) + len(FAR))

    pltpu.make_async_remote_copy(
        src_ref=all_sent, dst_ref=all_sent, send_sem=send_sem,
        recv_sem=z_sem, device_id=core_mate, device_id_type=MESH,
    ).wait_send()


def shards(
    contribution, left_basis, left_coef, right_coef, right_basis,
    left_rank, left_scale, right_rank, right_scale, left_owner, right_owner,
):
    smem = pl.BlockSpec(memory_space=pltpu.SMEM)
    hbm = pl.BlockSpec(memory_space=pl.ANY)
    unit = (RANK, WIDE)
    update = pl.pallas_call(
        kernel,
        out_shape=pltpu.VMEM((ROWS_OUT, COLS_OUT), F32),
        in_specs=[smem] * 6 + [hbm] * 4,
        out_specs=pl.BlockSpec(memory_space=pltpu.VMEM),
        scratch_shapes=[
            pltpu.VMEM((PANELS, 4) + unit, BF16),
            pltpu.VMEM((5, 2) + unit, BF16),
            pltpu.VMEM((5, 2) + unit, BF16),
            pltpu.VMEM((2, 3) + unit, BF16),
            pltpu.VMEM((2, 2) + unit, BF16),
            pltpu.VMEM((2, 4) + unit, BF16),
            pltpu.VMEM((2,) + unit, BF16),
            pltpu.VMEM((2,) + unit, BF16),
            pltpu.VMEM((PANELS, 4) + unit, BF16),
            pltpu.VMEM((2, PANELS) + unit, BF16),
            pltpu.VMEM((PANELS,) + unit, BF16),
            pltpu.VMEM((XS, 2) + unit, BF16),
            pltpu.VMEM((3, 2) + unit, BF16),
            pltpu.VMEM((HS, 32, WIDE), BF16),
            pltpu.VMEM((3, 32, WIDE), BF16),
            pltpu.VMEM((2, XS, HS, 32, WIDE), BF16),
            pltpu.VMEM((PANELS * RANK, WIDE), BF16),
            pltpu.VMEM((PANELS * RANK, COLS_OUT), BF16),
            pltpu.VMEM((PANELS * RANK, COLS_OUT), BF16),
            pltpu.VMEM((SENT,) + unit, BF16),
            pltpu.SemaphoreType.DMA((2,)),
            pltpu.SemaphoreType.DMA,
            pltpu.SemaphoreType.DMA((5,)),
            pltpu.SemaphoreType.DMA((2,)),
            pltpu.SemaphoreType.DMA,
            pltpu.SemaphoreType.DMA((2,)),
            pltpu.SemaphoreType.DMA((10,)),
            pltpu.SemaphoreType.DMA((4,)),
            pltpu.SemaphoreType.DMA((6,)),
        ],
        compiler_params=pltpu.CompilerParams(collective_id=0, has_side_effects=True),
    )(
        left_owner, right_owner, left_rank.T, left_scale.T, right_rank.T, right_scale.T,
        left_basis, left_coef, right_coef, right_basis,
    )
    return contribution - update


def solution(mesh):
    return jax.shard_map(
        shards,
        mesh=mesh,
        in_specs=(
            P("row", "col"),
            P(None, "col", None, "row"),
            P(None, "col", None, "row"),
            P(None, "row", None, "col"),
            P(None, "row", None, "col"),
            P(None, "row"),
            P(None, "row"),
            P(None, "col"),
            P(None, "col"),
            P(),
            P(),
        ),
        out_specs=P("row", "col"),
        check_vma=False,
    )
```

time: 46.4 us -> 45.1 us (0.972)
  the two profiles are of different devices: /device:TPU:14 before, /device:TPU:4 now
where the time goes in v4:
time: 45.1 us; the launch traced here: 44.9 us
  Pallas kernels  43.9 us (97%)
  other arithmetic  0.97 us (2%)
    pallas_call x1, Pallas kernels, shards(): pl.pallas_call(kernel, out_shape=pltpu.VMEM((ROWS_OUT, COLS_OUT), F32), i...  43.9 us
    sub x1, other arithmetic, shards(): return contribution - update  0.97 us

profile of v4, /device:TPU:4, one launch (start us, length us, event | category | flops | bytes accessed | tf_op | source)
XLA Modules:
  0.0 44.9 jit_solution(8364756277812833168)
XLA Ops:
  0.0 0.0 copy-start
  0.0 43.9 %shard_map.109 = f32[256,768]{1,0:T(8,128)S(1)} custom-call(s32[8]{0:T(128)} %lowner.1, s32[8]{0:T(128)} %rowner.1, s32[1,8]{1,0:T(1,128)} %bitcast.4, f32[1,8]{1,0:T(1,128)} %bitcast.5, s32[1,8]{1,0:T(1,128)} %bitcast.6, f32[1,8]{1,0:T(1,128)} %bitcast.7, bf16[8,1,64,256]{3,2,1,0:T(8,128)(2,1)} %lbasis.1, bf16[8,1,64,256]{3,2,1,0:T(8,128)(2,1)} %lcoef.1, ...), custom_call_target="tpu_custom_call" | custom-call | tf_op jit(solution)/shard_map/pallas_call | solution.py:286
  44.0 0.0 copy-done
  44.0 1.0 %sub.3 = f32[256,768]{1,0:T(8,128)} subtract(f32[256,768]{1,0:T(8,128)S(1)} %copy-done, f32[256,768]{1,0:T(8,128)S(1)} %shard_map.109) | non-fusion elementwise | flops 196608 | bytes 2359296 | tf_op jit(solution)/shard_map/sub | solution.py:327
Async XLA Ops:
  0.0 44.0 %copy-start = (f32[256,768]{1,0:T(8,128)S(1)}, f32[256,768]{1,0:T(8,128)}, u32[]{:S(2)}) copy-start(f32[256,768]{1,0:T(8,128)} %param.11) | copy-start | bytes 2359300

commit v5 on v4

--- a/solution.py
+++ b/solution.py
@@ -37,7 +37,7 @@
     own, yin, zout, passed, zin, near, hout, hin, right,
     lown, lother, lpick, lx, lhome, ly, left,
     basis, mid_high, mid_low, all_sent,
-    load_sem, send_sem, y_sem, p_sem, z_sem, n_sem, g_sem, f_sem, l_sem,
+    load_sem, send_sem, y_sem, p_sem, z_sem, n_sem, g_sem, f_sem, l_sem, h_sem,
 ):
     row, col = lax.axis_index("row"), lax.axis_index("col")
     z, q = row // 2, lax.rem(row, 2)
@@ -52,7 +52,7 @@
     y_mate, core_mate = (z * 2 + 1 - q, col), at_col(x, h, 1 - core)
     x_peers = [at_col(ring(x + d, XS), h, core) for d in (1, 2, 3)]
     h_peers = [at_col(x, ring(h + d, HS), core) for d in (1, 2, 3)]
-    everyone = [at_z(o) for o in FAR_FIRST + (1, 7)] + [y_mate, core_mate] + x_peers + h_peers
+    everyone = [at_z(o) for o in (1, -1, 2, -2)] + [y_mate, core_mate] + x_peers + [h_peers[0], h_peers[2]]
 
     for u in (1, 2, 3):
         columns = pl.ds(WIDE * (u - 1), WIDE)
@@ -92,6 +92,7 @@
 
     def left_h():
         wait(lx, l_sem.at[1])
+        pl.semaphore_wait(h_sem, 1)
         for i in range(2):
             away = ring(x - lowner[2 * x + i] // 8, XS)
             value = lpick[x, i]
@@ -132,34 +133,43 @@
     def keep_at(offset, e):
         return right.at[ring(z + offset, ZS), 2 * q + e]
 
-    def paired(offset):
+    def swap(offset):
+        slot = FAR_FIRST.index(offset)
+        for e in (0, 1):
+            unit = own.at[ring(z + offset, ZS), 2 * (1 - q) + e]
+            send(unit, yin.at[slot, e], y_sem.at[slot, e], y_mate)
+
+    def paired(offset, e):
         panel, slot = ring(z + offset, ZS), FAR_FIRST.index(offset)
-        wait(yin.at[slot], y_sem.at[slot])
+        wait(yin.at[slot, e], y_sem.at[slot, e])
         mine = lax.rem(rowner[panel], 2) == q
-        return jnp.where(mine, own[panel, stay], yin[slot])
+        return jnp.where(mine, own[panel, 2 * q + e], yin[slot, e])
 
     def begin(offset):
         slot = FAR_FIRST.index(offset)
-        zout[slot] = paired(offset)
-        if offset == 4:
-            for e, to in ((0, 2), (1, -2)):
-                send(zout.at[slot, e], passed.at[e, 2], p_sem.at[e], at_z(to))
-        else:
-            way, to = (0, 1) if offset == 3 else (1, -1)
-            send(zout.at[slot], passed.at[way, pl.ds(0, 2)], p_sem.at[way], at_z(to))
-
-    def merge(way):
-        offset = (2, 6)[way]
-        slot = FAR_FIRST.index(offset)
-        panel = ring(z + offset, ZS)
-        value = paired(offset)
-        wait(passed.at[way], p_sem.at[way])
-        away = ring(panel - rowner[panel] // 2, ZS)
-        value = jnp.where(away == (3, 5)[way], passed[way, 0:2], value)
-        zout[slot] = value
-        zout[slot, way] = jnp.where(away == 4, passed[way, 2], value[way])
-        for e in (way, 1 - way):
-            send(zout.at[slot, e], zin.at[way, e], z_sem, at_z((2, -2)[way]))
+        for e in (0, 1) if offset != 5 else (1, 0):
+            zout[slot, e] = paired(offset, e)
+            way = e if offset == 4 else 0 if offset == 3 else 1
+            place = 2 if offset == 4 else int(e == way)
+            far = 2 if offset == 4 else 1
+            send(zout.at[slot, e], passed.at[way, place], p_sem.at[way, int(e == way)], at_z((far, -far)[way]))
+
+    def merge(e):
+        for way, unit in ((0, e), (1, 1 - e)):
+            offset = (2, 6)[way]
+            slot = FAR_FIRST.index(offset)
+            panel = ring(z + offset, ZS)
+            value = paired(offset, unit)
+            away = ring(panel - rowner[panel] // 2, ZS)
+            if unit == way:
+                wait(passed.at[way, pl.ds(1, 2)], p_sem.at[way, 1])
+                value = jnp.where(away == (3, 5)[way], passed[way, 1], value)
+                value = jnp.where(away == 4, passed[way, 2], value)
+            else:
+                wait(passed.at[way, 0], p_sem.at[way, 0])
+                value = jnp.where(away == (3, 5)[way], passed[way, 0], value)
+            zout[slot, unit] = value
+            send(zout.at[slot, unit], zin.at[way, unit], z_sem, at_z((2, -2)[way]))
 
     source = ring(z - rowner[z] // 2, ZS)
 
@@ -182,8 +192,9 @@
 
     wait(own, load_sem.at[0])
     pl.semaphore_wait(barrier, len(everyone))
-    for slot, o in enumerate(FAR_FIRST):
-        send(own.at[ring(z + o, ZS), leave], yin.at[slot], y_sem.at[slot], y_mate)
+    pl.semaphore_signal(h_sem, inc=1, device_id=h_peers[0], device_id_type=MESH)
+    for o in FAR_FIRST[:3]:
+        swap(o)
     for i, d in enumerate((1, -1)):
         panel = ring(z + d, ZS)
         for units in (leave, stay):
@@ -191,7 +202,10 @@
     wait(lown, load_sem.at[1])
     left_core()
     left_x()
-    for o in FAR_FIRST[:3]:
+    begin(FAR_FIRST[0])
+    for o in FAR_FIRST[3:]:
+        swap(o)
+    for o in FAR_FIRST[1:3]:
         begin(o)
     wait(near, n_sem.at[0])
     hout[...] = near_pick(leave)
@@ -212,9 +226,6 @@
         forward(0, e)
         relay(0, e, 2)
         relay(0, 1 - e, -2)
-    for e in (0, 1):
-        relay(0, e, 1)
-        relay(0, 1 - e, -1)
     left_xback()
     for turn in (0, 1):
         for o, step, e in ((6, 1, turn), (2, -1, 1 - turn)):
@@ -223,6 +234,9 @@
                 relay(o, e, 2 * step)
             relay(o, e, step)
             forward(o, e)
+    for e in (0, 1):
+        relay(0, e, 1)
+        relay(0, 1 - e, -1)
     other = right.at[z, leave]
     wait(other, f_sem.at[F_SLOT[0]])
     for d in (1, -1):
@@ -311,13 +325,14 @@
             pltpu.VMEM((SENT,) + unit, BF16),
             pltpu.SemaphoreType.DMA((2,)),
             pltpu.SemaphoreType.DMA,
-            pltpu.SemaphoreType.DMA((5,)),
-            pltpu.SemaphoreType.DMA((2,)),
+            pltpu.SemaphoreType.DMA((5, 2)),
+            pltpu.SemaphoreType.DMA((2, 2)),
             pltpu.SemaphoreType.DMA,
             pltpu.SemaphoreType.DMA((2,)),
             pltpu.SemaphoreType.DMA((10,)),
             pltpu.SemaphoreType.DMA((4,)),
             pltpu.SemaphoreType.DMA((6,)),
+            pltpu.SemaphoreType.REGULAR,
         ],
         compiler_params=pltpu.CompilerParams(collective_id=0, has_side_effects=True),
     )(

time: 45.1 us -> 43.4 us (0.962)
  the two profiles are of different devices: /device:TPU:4 before, /device:TPU:18 now
where the time goes in v5:
time: 43.4 us; the launch traced here: 43.2 us
  Pallas kernels  42.2 us (97%)
  other arithmetic  0.97 us (2%)
    pallas_call x1, Pallas kernels, shards(): pl.pallas_call(kernel, out_shape=pltpu.VMEM((ROWS_OUT, COLS_OUT), F32), i...  42.2 us
    sub x1, other arithmetic, shards(): return contribution - update  0.97 us

profile of v5, /device:TPU:18, one launch (start us, length us, event | category | flops | bytes accessed | tf_op | source)
XLA Modules:
  0.0 43.2 jit_solution(8151432711649492402)
XLA Ops:
  0.0 0.0 copy-start
  0.0 42.2 %shard_map.109 = f32[256,768]{1,0:T(8,128)S(1)} custom-call(s32[8]{0:T(128)} %lowner.1, s32[8]{0:T(128)} %rowner.1, s32[1,8]{1,0:T(1,128)} %bitcast.4, f32[1,8]{1,0:T(1,128)} %bitcast.5, s32[1,8]{1,0:T(1,128)} %bitcast.6, f32[1,8]{1,0:T(1,128)} %bitcast.7, bf16[8,1,64,256]{3,2,1,0:T(8,128)(2,1)} %lbasis.1, bf16[8,1,64,256]{3,2,1,0:T(8,128)(2,1)} %lcoef.1, ...), custom_call_target="tpu_custom_call" | custom-call | tf_op jit(solution)/shard_map/pallas_call | solution.py:300
  42.3 0.0 copy-done
  42.3 1.0 %sub.3 = f32[256,768]{1,0:T(8,128)} subtract(f32[256,768]{1,0:T(8,128)S(1)} %copy-done, f32[256,768]{1,0:T(8,128)S(1)} %shard_map.109) | non-fusion elementwise | flops 196608 | bytes 2359296 | tf_op jit(solution)/shard_map/sub | solution.py:342
Async XLA Ops:
  0.0 42.3 %copy-start = (f32[256,768]{1,0:T(8,128)S(1)}, f32[256,768]{1,0:T(8,128)}, u32[]{:S(2)}) copy-start(f32[256,768]{1,0:T(8,128)} %param.11) | copy-start | bytes 2359300

commit v6 on v5

--- a/solution.py
+++ b/solution.py
@@ -52,7 +52,7 @@
     y_mate, core_mate = (z * 2 + 1 - q, col), at_col(x, h, 1 - core)
     x_peers = [at_col(ring(x + d, XS), h, core) for d in (1, 2, 3)]
     h_peers = [at_col(x, ring(h + d, HS), core) for d in (1, 2, 3)]
-    everyone = [at_z(o) for o in (1, -1, 2, -2)] + [y_mate, core_mate] + x_peers + [h_peers[0], h_peers[2]]
+    everyone = [at_z(o) for o in (1, -1, 2, -2)] + [y_mate, core_mate] + x_peers
 
     for u in (1, 2, 3):
         columns = pl.ds(WIDE * (u - 1), WIDE)
@@ -61,9 +61,21 @@
     pltpu.make_async_copy(lbasis.at[:, 0], lown.at[0], load_sem.at[1]).start()
     pltpu.make_async_copy(lcoef.at[:, 0], lown.at[1], load_sem.at[1]).start()
 
+    def tell(sem, peer):
+        pl.semaphore_signal(sem, inc=1, device_id=peer, device_id_type=MESH)
+
+    h_next, h_last = h_peers[0], h_peers[2]
     barrier = pltpu.get_barrier_semaphore()
     for peer in everyone:
-        pl.semaphore_signal(barrier, inc=1, device_id=peer, device_id_type=MESH)
+        tell(barrier, peer)
+
+    @pl.when(h < HS - 1)
+    def _():
+        tell(barrier, h_next)
+
+    @pl.when(h > 0)
+    def _():
+        tell(barrier, h_last)
 
     def send(src, dst, sem, peer):
         pltpu.make_async_remote_copy(
@@ -92,7 +104,11 @@
 
     def left_h():
         wait(lx, l_sem.at[1])
-        pl.semaphore_wait(h_sem, 1)
+
+        @pl.when(jnp.logical_not(inner))
+        def _():
+            pl.semaphore_wait(h_sem, 2)
+
         for i in range(2):
             away = ring(x - lowner[2 * x + i] // 8, XS)
             value = lpick[x, i]
@@ -191,8 +207,14 @@
         wait(keep_at(offset, e), g_sem.at[G_SLOT[offset, e]])
 
     wait(own, load_sem.at[0])
-    pl.semaphore_wait(barrier, len(everyone))
-    pl.semaphore_signal(h_sem, inc=1, device_id=h_peers[0], device_id_type=MESH)
+    inner = (h > 0) & (h < HS - 1)
+    pl.semaphore_wait(barrier, len(everyone) + jnp.where(inner, 2, 1))
+
+    @pl.when(inner)
+    def _():
+        tell(h_sem, h_next)
+        tell(h_sem, h_last)
+
     for o in FAR_FIRST[:3]:
         swap(o)
     for i, d in enumerate((1, -1)):
@@ -203,6 +225,12 @@
     left_core()
     left_x()
     begin(FAR_FIRST[0])
+
+    @pl.when(inner)
+    def _():
+        pl.semaphore_wait(h_sem, 1)
+        tell(h_sem, (row, (x * 4 + jnp.where(h == 1, 0, HS - 1)) * 2 + core))
+
     for o in FAR_FIRST[3:]:
         swap(o)
     for o in FAR_FIRST[1:3]:

time: 43.4 us -> 43.2 us (level)
  the two profiles are of different devices: /device:TPU:18 before, /device:TPU:22 now
where the time goes in v6:
time: 43.2 us; the launch traced here: 43.1 us
  Pallas kernels  42.1 us (97%)
  other arithmetic  0.97 us (2%)
    pallas_call x1, Pallas kernels, shards(): pl.pallas_call(kernel, out_shape=pltpu.VMEM((ROWS_OUT, COLS_OUT), F32), i...  42.1 us
    sub x1, other arithmetic, shards(): return contribution - update  0.97 us

profile of v6, /device:TPU:22, one launch (start us, length us, event | category | flops | bytes accessed | tf_op | source)
XLA Modules:
  0.0 43.1 jit_solution(8854743741391228333)
XLA Ops:
  0.0 0.0 copy-start
  0.0 42.1 %shard_map.109 = f32[256,768]{1,0:T(8,128)S(1)} custom-call(s32[8]{0:T(128)} %lowner.1, s32[8]{0:T(128)} %rowner.1, s32[1,8]{1,0:T(1,128)} %bitcast.4, f32[1,8]{1,0:T(1,128)} %bitcast.5, s32[1,8]{1,0:T(1,128)} %bitcast.6, f32[1,8]{1,0:T(1,128)} %bitcast.7, bf16[8,1,64,256]{3,2,1,0:T(8,128)(2,1)} %lbasis.1, bf16[8,1,64,256]{3,2,1,0:T(8,128)(2,1)} %lcoef.1, ...), custom_call_target="tpu_custom_call" | custom-call | tf_op jit(solution)/shard_map/pallas_call | solution.py:328
  42.1 0.0 copy-done
  42.1 1.0 %sub.3 = f32[256,768]{1,0:T(8,128)} subtract(f32[256,768]{1,0:T(8,128)S(1)} %copy-done, f32[256,768]{1,0:T(8,128)S(1)} %shard_map.109) | non-fusion elementwise | flops 196608 | bytes 2359296 | tf_op jit(solution)/shard_map/sub | solution.py:370
Async XLA Ops:
  0.0 42.1 %copy-start = (f32[256,768]{1,0:T(8,128)S(1)}, f32[256,768]{1,0:T(8,128)}, u32[]{:S(2)}) copy-start(f32[256,768]{1,0:T(8,128)} %param.11) | copy-start | bytes 2359300
